TPU v7x, 32 devices: a whole 2x2x4 slice. The times are simulated.
32 devices in a mesh: gx: 4 (over z), gy: 8 (over y, x, core).
Axes of the slice: x: 2, y: 2, z: 4, core: 2. Of those that a mesh axis runs over, the one named last changes fastest.
Arguments:
- patches: bfloat16 [39168, 768], P(('gx', 'gy')), may hold values from -6 to 6
- lengths: int32 [32], P(('gx', 'gy')), may hold values from 122 to 1224, as said below
- cotangent: bfloat16 [39168, 768], P(('gx', 'gy')), may hold values from -6 to 6
- w_qkv: bfloat16 [768, 2304], P('gx', 'gy'), may hold values from -0.21875 to 0.21875
- w_out: bfloat16 [768, 768], P('gx', 'gy'), may hold values from -4 to 4
- w_up: bfloat16 [768, 3072], P('gx', 'gy'), may hold values from -0.21875 to 0.21875
- w_down: bfloat16 [3072, 768], P('gx', 'gy'), may hold values from -0.109375 to 0.109375
- bias_q: bfloat16 [768], P(('gx', 'gy')), may hold values from -3 to 3
- bias_v: bfloat16 [768], P(('gx', 'gy')), may hold values from -3 to 3
- bias_o: bfloat16 [768], P(('gx', 'gy')), may hold values from -1.75 to 1.75
- bias_up: bfloat16 [3072], P(('gx', 'gy')), may hold values from -3 to 3
- bias_down: bfloat16 [768], P(('gx', 'gy')), may hold values from -1.75 to 1.75
- gain_one: bfloat16 [768], P(('gx', 'gy')), may hold values from 0.5 to 1.5
- shift_one: bfloat16 [768], P(('gx', 'gy')), may hold values from -1.75 to 1.75
- gain_two: bfloat16 [768], P(('gx', 'gy')), may hold values from 0.5 to 1.5
- shift_two: bfloat16 [768], P(('gx', 'gy')), may hold values from -1.75 to 1.75
Outputs:
- out_rows: bfloat16 [39168, 768], P(('gx', 'gy'))
- grad_rows: float32 [39168, 768], P(('gx', 'gy'))
- grad_w_qkv: float32 [768, 2304], P('gx', 'gy')
- grad_w_out: float32 [768, 768], P('gx', 'gy')
- grad_w_up: float32 [768, 3072], P('gx', 'gy')
- grad_w_down: float32 [3072, 768], P('gx', 'gy')
- grad_bias_q: float32 [768], P(('gx', 'gy'))
- grad_bias_v: float32 [768], P(('gx', 'gy'))
- grad_bias_o: float32 [768], P(('gx', 'gy'))
- grad_bias_up: float32 [3072], P(('gx', 'gy'))
- grad_bias_down: float32 [768], P(('gx', 'gy'))
- grad_gain_one: float32 [768], P(('gx', 'gy'))
- grad_shift_one: float32 [768], P(('gx', 'gy'))
- grad_gain_two: float32 [768], P(('gx', 'gy'))
- grad_shift_two: float32 [768], P(('gx', 'gy'))
Inputs may be any that keep to these rules, and one draw needn't show every extreme that they name: `lengths`: each clip's true patch count; some clip fills all 1224 slots and some clip has 122 patches in every draw.
All inputs are finite; a program needn't handle non-finite values.
Results may differ from a plain program's by a relative error of at most 0.02.
Values may be sent and summed in bfloat16 or wider, within the bound.
No kernel may reach another device: no remote copies, remote signals or barrier semaphores. Data moves between devices by JAX's collectives and lax.ppermute only.
A program may use at most 192 MiB of HBM per device.

v0:
```python
import jax
import jax.numpy as jnp
from jax import lax
from jax.sharding import PartitionSpec as P

HEADS = 12
HEAD_DIM = 64
EPSILON = 1e-06
NEG_FILL = -1e30


def layer_norm(values, gain_vec, shift_vec):
    centre = values - jnp.mean(values, axis=-1, keepdims=True)
    spread = jnp.mean(centre * centre, axis=-1, keepdims=True)
    return centre * lax.rsqrt(spread + EPSILON) * gain_vec + shift_vec


def exact_gelu(values):
    return jax.nn.gelu(values, approximate=False)


def to_blocks(columns, clip_count, pair_count):
    slot_count = columns.shape[0] // clip_count
    pair_width = columns.shape[1] // pair_count
    shaped = columns.reshape(clip_count, slot_count, pair_count, pair_width)
    return jnp.transpose(shaped, (0, 2, 1, 3)).reshape(
        clip_count * pair_count, slot_count, pair_width
    )


def from_blocks(blocks_in, clip_count, pair_count):
    slot_count = blocks_in.shape[1]
    pair_width = blocks_in.shape[2]
    shaped = blocks_in.reshape(clip_count, pair_count, slot_count, pair_width)
    return jnp.transpose(shaped, (0, 2, 1, 3)).reshape(
        clip_count * slot_count, pair_count * pair_width
    )


def block_scores(queries, key_rows, length):
    slot_count = queries.shape[0]
    query_heads = queries.reshape(slot_count, 2, HEAD_DIM)
    key_heads = key_rows.reshape(slot_count, 2, HEAD_DIM)
    scores = jnp.einsum(
        "qhd,khd->hqk", query_heads, key_heads, preferred_element_type=jnp.float32
    ) * HEAD_DIM ** (-0.5)
    live_keys = jnp.arange(slot_count) < length
    return (jnp.where(live_keys[None, None, :], scores, NEG_FILL), query_heads, key_heads)


def attend(block_in):
    queries, key_rows, values, length = block_in
    scores, query_heads, key_heads = block_scores(queries, key_rows, length)
    maximum = jnp.max(scores, axis=-1, keepdims=True)
    exponent = jnp.exp(scores - maximum)
    summed = jnp.sum(exponent, axis=-1, keepdims=True)
    weights = (exponent / summed).astype(jnp.bfloat16)
    value_heads = values.reshape(values.shape[0], 2, HEAD_DIM)
    mixed_heads = jnp.einsum(
        "hqk,khd->qhd", weights, value_heads, preferred_element_type=jnp.float32
    )
    return (
        mixed_heads.reshape(queries.shape[0], 2 * HEAD_DIM),
        (maximum + jnp.log(summed))[..., 0],
    )


def attend_back(block_in):
    queries, key_rows, values, grad_out, log_total, length = block_in
    slot_count = queries.shape[0]
    scores, query_heads, key_heads = block_scores(queries, key_rows, length)
    weights = jnp.exp(scores - log_total[..., None])
    value_heads = values.reshape(slot_count, 2, HEAD_DIM)
    grad_heads = grad_out.reshape(slot_count, 2, HEAD_DIM)
    d_weights = jnp.einsum(
        "qhd,khd->hqk", grad_heads, value_heads, preferred_element_type=jnp.float32
    )
    d_values = jnp.einsum(
        "hqk,qhd->khd", weights.astype(jnp.bfloat16), grad_heads, preferred_element_type=jnp.float32
    )
    row_dots = jnp.sum(weights * d_weights, axis=-1, keepdims=True)
    d_scores = (weights * (d_weights - row_dots)).astype(jnp.bfloat16)
    d_queries = jnp.einsum(
        "hqk,khd->qhd", d_scores, key_heads, preferred_element_type=jnp.float32
    ) * HEAD_DIM ** (-0.5)
    d_keys = jnp.einsum(
        "hqk,qhd->khd", d_scores, query_heads, preferred_element_type=jnp.float32
    ) * HEAD_DIM ** (-0.5)
    return (
        d_queries.reshape(slot_count, 2 * HEAD_DIM),
        d_keys.reshape(slot_count, 2 * HEAD_DIM),
        d_values.reshape(slot_count, 2 * HEAD_DIM),
    )


def per_device(
    patches,
    lengths,
    cotangent,
    w_qkv,
    w_out,
    w_up,
    w_down,
    bias_q,
    bias_v,
    bias_o,
    bias_up,
    bias_down,
    gain_one,
    shift_one,
    gain_two,
    shift_two,
):
    by_cols = (
        lax.all_gather(w_qkv, "gy", axis=1, tiled=True),
        lax.all_gather(w_out, "gy", axis=1, tiled=True),
        lax.all_gather(w_up, "gy", axis=1, tiled=True),
        lax.all_gather(w_down, "gy", axis=1, tiled=True),
        lax.all_gather(bias_q, "gy", axis=0, tiled=True),
        lax.all_gather(bias_v, "gy", axis=0, tiled=True),
        lax.all_gather(bias_o, "gy", axis=0, tiled=True),
        lax.all_gather(bias_up, "gy", axis=0, tiled=True),
        lax.all_gather(bias_down, "gy", axis=0, tiled=True),
        lax.all_gather(gain_one, "gy", axis=0, tiled=True),
        lax.all_gather(shift_one, "gy", axis=0, tiled=True),
        lax.all_gather(gain_two, "gy", axis=0, tiled=True),
        lax.all_gather(shift_two, "gy", axis=0, tiled=True),
    )
    gathered = (
        lax.all_gather(by_cols[0], "gx", axis=0, tiled=True),
        lax.all_gather(by_cols[1], "gx", axis=0, tiled=True),
        lax.all_gather(by_cols[2], "gx", axis=0, tiled=True),
        lax.all_gather(by_cols[3], "gx", axis=0, tiled=True),
        lax.all_gather(by_cols[4], "gx", axis=0, tiled=True),
        lax.all_gather(by_cols[5], "gx", axis=0, tiled=True),
        lax.all_gather(by_cols[6], "gx", axis=0, tiled=True),
        lax.all_gather(by_cols[7], "gx", axis=0, tiled=True),
        lax.all_gather(by_cols[8], "gx", axis=0, tiled=True),
        lax.all_gather(by_cols[9], "gx", axis=0, tiled=True),
        lax.all_gather(by_cols[10], "gx", axis=0, tiled=True),
        lax.all_gather(by_cols[11], "gx", axis=0, tiled=True),
        lax.all_gather(by_cols[12], "gx", axis=0, tiled=True),
    )
    mat_qkv, mat_out, mat_up, mat_down = (gathered[0], gathered[1], gathered[2], gathered[3])
    vec_q, vec_v, vec_o, vec_up, vec_down, gain_a, shift_a, gain_b, shift_b = [
        member.astype(jnp.float32) for member in gathered[4:]
    ]
    clip_count = lengths.shape[0]
    slot_count = patches.shape[0] // clip_count
    model_width = patches.shape[1]
    pair_count = HEADS // 2
    inputs32 = patches.astype(jnp.float32)
    normed, norm_pull = jax.vjp(layer_norm, inputs32, gain_a, shift_a)
    normed_low = normed.astype(jnp.bfloat16)
    bias_all = jnp.concatenate([vec_q, jnp.zeros_like(vec_q), vec_v])
    project = (jnp.dot(normed_low, mat_qkv, preferred_element_type=jnp.float32) + bias_all).astype(
        jnp.bfloat16
    )
    query_blocks = to_blocks(project[:, :model_width], clip_count, pair_count)
    key_blocks = to_blocks(project[:, model_width : 2 * model_width], clip_count, pair_count)
    value_blocks = to_blocks(project[:, 2 * model_width :], clip_count, pair_count)
    pair_lengths = jnp.repeat(lengths, pair_count)
    mixed_blocks, total_blocks = lax.map(
        attend, (query_blocks, key_blocks, value_blocks, pair_lengths)
    )
    mixed_low = from_blocks(mixed_blocks, clip_count, pair_count).astype(jnp.bfloat16)
    residual = inputs32 + jnp.dot(mixed_low, mat_out, preferred_element_type=jnp.float32) + vec_o
    normed_two, norm_pull_two = jax.vjp(layer_norm, residual, gain_b, shift_b)
    normed_two_low = normed_two.astype(jnp.bfloat16)
    inner_pre = jnp.dot(normed_two_low, mat_up, preferred_element_type=jnp.float32) + vec_up
    active, gelu_pull = jax.vjp(exact_gelu, inner_pre)
    active_low = active.astype(jnp.bfloat16)
    outputs = (
        residual + jnp.dot(active_low, mat_down, preferred_element_type=jnp.float32) + vec_down
    ).astype(jnp.bfloat16)
    regather_cols = (
        lax.all_gather(w_qkv, "gy", axis=1, tiled=True),
        lax.all_gather(w_out, "gy", axis=1, tiled=True),
        lax.all_gather(w_up, "gy", axis=1, tiled=True),
        lax.all_gather(w_down, "gy", axis=1, tiled=True),
    )
    regathered = (
        lax.all_gather(regather_cols[0], "gx", axis=0, tiled=True),
        lax.all_gather(regather_cols[1], "gx", axis=0, tiled=True),
        lax.all_gather(regather_cols[2], "gx", axis=0, tiled=True),
        lax.all_gather(regather_cols[3], "gx", axis=0, tiled=True),
    )
    back_qkv, back_out, back_up, back_down = (
        regathered[0],
        regathered[1],
        regathered[2],
        regathered[3],
    )
    live_rows = (
        (jnp.arange(slot_count)[None, :] < lengths[:, None]).astype(jnp.float32).reshape(-1, 1)
    )
    seed_grad = cotangent.astype(jnp.float32) * live_rows
    seed_low = seed_grad.astype(jnp.bfloat16)
    grad_bias_down = jnp.sum(seed_grad, axis=0)
    grad_w_down = jnp.einsum("tf,td->fd", active_low, seed_low, preferred_element_type=jnp.float32)
    d_active = jnp.einsum("td,fd->tf", seed_low, back_down, preferred_element_type=jnp.float32)
    d_inner = gelu_pull(d_active)[0].astype(jnp.bfloat16)
    grad_bias_up = jnp.sum(d_inner.astype(jnp.float32), axis=0)
    grad_w_up = jnp.einsum("td,tf->df", normed_two_low, d_inner, preferred_element_type=jnp.float32)
    d_normed_two = jnp.einsum("tf,df->td", d_inner, back_up, preferred_element_type=jnp.float32)
    d_resid_norm, grad_gain_two, grad_shift_two = norm_pull_two(d_normed_two)
    d_residual = seed_grad + d_resid_norm
    grad_bias_o = jnp.sum(d_residual, axis=0)
    d_branch = d_residual.astype(jnp.bfloat16)
    grad_w_out = jnp.einsum("te,td->ed", mixed_low, d_branch, preferred_element_type=jnp.float32)
    d_mixed = jnp.einsum(
        "td,ed->te", d_branch, back_out, preferred_element_type=jnp.float32
    ).astype(jnp.bfloat16)
    grad_blocks = to_blocks(d_mixed, clip_count, pair_count)
    d_queries, d_keys, d_values = lax.map(
        attend_back,
        (query_blocks, key_blocks, value_blocks, grad_blocks, total_blocks, pair_lengths),
    )
    d_project = jnp.concatenate(
        [
            from_blocks(d_queries, clip_count, pair_count),
            from_blocks(d_keys, clip_count, pair_count),
            from_blocks(d_values, clip_count, pair_count),
        ],
        axis=1,
    ).astype(jnp.bfloat16)
    column_sums = jnp.sum(d_project.astype(jnp.float32), axis=0)
    grad_bias_q = column_sums[:model_width]
    grad_bias_v = column_sums[2 * model_width :]
    grad_w_qkv = jnp.einsum("td,te->de", normed_low, d_project, preferred_element_type=jnp.float32)
    d_normed = jnp.einsum("te,de->td", d_project, back_qkv, preferred_element_type=jnp.float32)
    d_input_norm, grad_gain_one, grad_shift_one = norm_pull(d_normed)
    grad_rows = d_residual + d_input_norm
    section_one = (
        lax.psum_scatter(
            grad_w_qkv.astype(jnp.bfloat16), "gx", scatter_dimension=0, tiled=True
        ).astype(jnp.float32),
        lax.psum_scatter(
            grad_w_out.astype(jnp.bfloat16), "gx", scatter_dimension=0, tiled=True
        ).astype(jnp.float32),
        lax.psum_scatter(
            grad_w_up.astype(jnp.bfloat16), "gx", scatter_dimension=0, tiled=True
        ).astype(jnp.float32),
        lax.psum_scatter(
            grad_w_down.astype(jnp.bfloat16), "gx", scatter_dimension=0, tiled=True
        ).astype(jnp.float32),
        lax.psum_scatter(
            grad_bias_q.astype(jnp.bfloat16), "gx", scatter_dimension=0, tiled=True
        ).astype(jnp.float32),
        lax.psum_scatter(
            grad_bias_v.astype(jnp.bfloat16), "gx", scatter_dimension=0, tiled=True
        ).astype(jnp.float32),
        lax.psum_scatter(
            grad_bias_o.astype(jnp.bfloat16), "gx", scatter_dimension=0, tiled=True
        ).astype(jnp.float32),
        lax.psum_scatter(
            grad_bias_up.astype(jnp.bfloat16), "gx", scatter_dimension=0, tiled=True
        ).astype(jnp.float32),
        lax.psum_scatter(
            grad_bias_down.astype(jnp.bfloat16), "gx", scatter_dimension=0, tiled=True
        ).astype(jnp.float32),
        lax.psum_scatter(
            grad_gain_one.astype(jnp.bfloat16), "gx", scatter_dimension=0, tiled=True
        ).astype(jnp.float32),
        lax.psum_scatter(
            grad_shift_one.astype(jnp.bfloat16), "gx", scatter_dimension=0, tiled=True
        ).astype(jnp.float32),
        lax.psum_scatter(
            grad_gain_two.astype(jnp.bfloat16), "gx", scatter_dimension=0, tiled=True
        ).astype(jnp.float32),
        lax.psum_scatter(
            grad_shift_two.astype(jnp.bfloat16), "gx", scatter_dimension=0, tiled=True
        ).astype(jnp.float32),
    )
    reduced = (
        lax.psum_scatter(
            section_one[0].astype(jnp.bfloat16), "gy", scatter_dimension=1, tiled=True
        ).astype(jnp.float32),
        lax.psum_scatter(
            section_one[1].astype(jnp.bfloat16), "gy", scatter_dimension=1, tiled=True
        ).astype(jnp.float32),
        lax.psum_scatter(
            section_one[2].astype(jnp.bfloat16), "gy", scatter_dimension=1, tiled=True
        ).astype(jnp.float32),
        lax.psum_scatter(
            section_one[3].astype(jnp.bfloat16), "gy", scatter_dimension=1, tiled=True
        ).astype(jnp.float32),
        lax.psum_scatter(
            section_one[4].astype(jnp.bfloat16), "gy", scatter_dimension=0, tiled=True
        ).astype(jnp.float32),
        lax.psum_scatter(
            section_one[5].astype(jnp.bfloat16), "gy", scatter_dimension=0, tiled=True
        ).astype(jnp.float32),
        lax.psum_scatter(
            section_one[6].astype(jnp.bfloat16), "gy", scatter_dimension=0, tiled=True
        ).astype(jnp.float32),
        lax.psum_scatter(
            section_one[7].astype(jnp.bfloat16), "gy", scatter_dimension=0, tiled=True
        ).astype(jnp.float32),
        lax.psum_scatter(
            section_one[8].astype(jnp.bfloat16), "gy", scatter_dimension=0, tiled=True
        ).astype(jnp.float32),
        lax.psum_scatter(
            section_one[9].astype(jnp.bfloat16), "gy", scatter_dimension=0, tiled=True
        ).astype(jnp.float32),
        lax.psum_scatter(
            section_one[10].astype(jnp.bfloat16), "gy", scatter_dimension=0, tiled=True
        ).astype(jnp.float32),
        lax.psum_scatter(
            section_one[11].astype(jnp.bfloat16), "gy", scatter_dimension=0, tiled=True
        ).astype(jnp.float32),
        lax.psum_scatter(
            section_one[12].astype(jnp.bfloat16), "gy", scatter_dimension=0, tiled=True
        ).astype(jnp.float32),
    )
    return (
        outputs,
        grad_rows,
        reduced[0],
        reduced[1],
        reduced[2],
        reduced[3],
        reduced[4],
        reduced[5],
        reduced[6],
        reduced[7],
        reduced[8],
        reduced[9],
        reduced[10],
        reduced[11],
        reduced[12],
    )


def solution(mesh):
    in_specs = (
        P(("gx", "gy"), None),
        P(("gx", "gy")),
        P(("gx", "gy"), None),
        P("gx", "gy"),
        P("gx", "gy"),
        P("gx", "gy"),
        P("gx", "gy"),
        P(("gx", "gy")),
        P(("gx", "gy")),
        P(("gx", "gy")),
        P(("gx", "gy")),
        P(("gx", "gy")),
        P(("gx", "gy")),
        P(("gx", "gy")),
        P(("gx", "gy")),
        P(("gx", "gy")),
    )
    out_specs = (
        P(("gx", "gy"), None),
        P(("gx", "gy"), None),
        P("gx", "gy"),
        P("gx", "gy"),
        P("gx", "gy"),
        P("gx", "gy"),
        P(("gx", "gy")),
        P(("gx", "gy")),
        P(("gx", "gy")),
        P(("gx", "gy")),
        P(("gx", "gy")),
        P(("gx", "gy")),
        P(("gx", "gy")),
        P(("gx", "gy")),
        P(("gx", "gy")),
    )
    return jax.shard_map(
        per_device, mesh=mesh, in_specs=in_specs, out_specs=out_specs, check_vma=False
    )
```

profile of v0, /device:TPU:0, one launch (start us, length us, event | category | flops | bytes accessed | tf_op | source)
XLA Modules:
  0.0 970.7 jit_solution(14444285091718010703)
XLA Ops:
  10.0 13.0 %all_gather.90 = bf16[192,2304]{0,1:T(8,128)(2,1)S(1)} all-gather(bf16[192,288]{0,1:T(8,128)(2,1)S(1)} %copy.64), channel_id=1, replica_groups=mesh['gx'=4,'gy'=8] {'gy'}, dimensions={1}, use_global_device_ids=true | all-gather | bytes 995328 | tf_op jit(solution)/shard_map/all_gather | solution.py:115
  24.5 10.5 %all_gather.96 = bf16[192,768]{0,1:T(8,128)(2,1)S(1)} all-gather(bf16[192,96]{0,1:T(8,128)(2,1)S(1)} %copy.69), channel_id=1, replica_groups=mesh['gx'=4,'gy'=8] {'gy'}, dimensions={1}, use_global_device_ids=true | all-gather | bytes 331776 | tf_op jit(solution)/shard_map/all_gather | solution.py:116
  42.0 13.4 %all-reduce.36 = (bf16[768]{0:T(1024)(128)(2,1)S(1)}, bf16[192]{0:T(256)(128)(2,1)S(1)}, bf16[192]{0:T(256)(128)(2,1)S(1)}, bf16[192]{0:T(256)(128)(2,1)S(1)}, b...) all-reduce(bf16[768]{0:T(1024)(128)(2,1)S(1)} %dynamic-update-slice, ...), channel_id=1, replica_groups=mesh['gx'=4,'gy'=8] {'gy'}, use_global_device_ids=true, to_apply=%add.14 | all-reduce | flops 2112 | bytes 8448
  56.9 19.1 %all-reduce.38 = (bf16[768]{0:T(1024)(128)(2,1)S(1)}, bf16[768]{0:T(1024)(128)(2,1)S(1)}, bf16[768]{0:T(1024)(128)(2,1)S(1)}, bf16[768]{0:T(1024)(128)(2,1)S(1)}...) all-reduce(bf16[768]{0:T(1024)(128)(2,1)S(1)} %dynamic-update-slice, ...), channel_id=1, replica_groups=mesh['gx'=4,'gy'=8] {'gx'}, use_global_device_ids=true, to_apply=%add.7 | all-reduce | flops 5376 | bytes 21504
  76.8 13.6 %all-gather = bf16[4,1,768]{2,1,0:T(2,128)(2,1)S(1)} all-gather(bf16[1,1,768]{2,1,0:T(2,128)(2,1)S(1)} %reshape.302), channel_id=1, replica_groups=mesh['gx'=4,'gy'=8] {'gx'}, dimensions={0}, use_global_device_ids=true | all-gather | bytes 7680 | tf_op jit(solution)/shard_map/all_gather | solution.py:137
  93.0 43.1 %all-gather.8.cloned.1.call-done = bf16[768,2304]{1,0:T(8,128)(2,1)} async-done(((bf16[192,2304]{1,0:T(8,128)(2,1)}), bf16[768,2304]{1,0:T(8,128)(2,1)}) %all-gather.8.cloned.1.call-update) | async-done | bytes 3538960 | tf_op jit(solution)/shard_map/all_gather | solution.py:130
  136.1 7.4 fusion.14
  159.5 65.9 %while.26 = (s32[]{:T(128)}, bf16[6,1224,128]{1,2,0:T(8,128)(2,1)}, f32[6,2,1224]{2,1,0:T(2,128)}, bf16[6,1224,128]{1,2,0:T(8,128)(2,1)}, s32[6]{0:T(128)S(1)}, ...) while((s32[]{:T(128)}, bf16[6,1224,128]{1,2,0:T(8,128)(2,1)}, ...), condition=%wide.region_5.6_spmd, body=%wide.region_2.5_spmd.sunk | while | flops 791035712 | bytes 39813052 | solution.py:163
  231.7 25.5 %all-gather.14.cloned.1.call-done = bf16[768,3072]{1,0:T(8,128)(2,1)} async-done(((bf16[192,3072]{1,0:T(8,128)(2,1)}), bf16[768,3072]{1,0:T(8,128)(2,1)}) %all-gather.14.cloned.1.call-update) | async-done | bytes 4718608 | tf_op jit(solution)/shard_map/all_gather | solution.py:132
  257.2 42.4 %multiply_convert_fusion.1 = (bf16[1224,3072]{1,0:T(8,128)(2,1)}, f32[1224,3072]{1,0:T(8,128)}, f32[1224,3072]{1,0:T(8,128)}) fusion(f32[3072]{0:T(1024)S(1)} %bitcast.196, bf16[768,3072]{1,0:T(8,128)(2,1)} %all-gather.14.cloned.1.call-done, f32[1224,768]{1,0:T(8,128)} %copy-done.2, f32[768]{0:T(1024)S(1)} %convert_element_type.206, ...), kind=kOutput, calls=%fused_computation.34 | convolution fusion | flops 6028425216 | bytes 46108224 | tf_op jit(solution)/shard_map/dot_general | solution.py:170
  299.6 46.9 %all-gather.18.cloned.1.call-done = bf16[3072,768]{0,1:T(8,128)(2,1)} async-done(((bf16[768,768]{0,1:T(8,128)(2,1)}), bf16[3072,768]{0,1:T(8,128)(2,1)}) %all-gather.18.cloned.1.call-update) | async-done | bytes 4718608 | tf_op jit(solution)/shard_map/all_gather | solution.py:133
  346.5 19.9 %fusion.53 = (bf16[3072]{0:T(1024)(128)(2,1)}, bf16[1224,3072]{1,0:T(8,128)(2,1)}) fusion(f32[1224,3072]{1,0:T(8,128)} %get-tuple-element.252, f32[1224,3072]{1,0:T(8,128)} %get-tuple-element.273, bf16[3072,768]{0,1:T(8,128)(2,1)} %all-gather.18.cloned.1.call-done, bf16[1224,768]{1,0:T(8,128)(2,1)S(1)} %copy-done.7, f32[1224]{0:T(1024)S(1)} %copy-done.21), kind=kOutput, calls=%fused_computation.122 | convolution fusion | flops 5834775552 | bytes 44210976 | tf_op jit(solution)/shard_map/td,fd->tf/dot_general | solution.py:201
  366.4 12.7 %multiply_reduce_fusion.1 = (bf16[768]{0:T(1024)(128)(2,1)}, f32[1224]{0:T(1024)S(1)}, bf16[768]{0:T(1024)(128)(2,1)}, f32[1224,768]{1,0:T(8,128)S(1)}) fusion(f32[1224,768]{1,0:T(8,128)} %copy-done.2, f32[1224]{0:T(1024)S(1)} %fusion.37, f32[1224]{0:T(1024)S(1)} %broadcast_multiply_fusion, f32[768]{0:T(1024)S(1)} %convert_element_type.205, ...), kind=kOutput, calls=%fused_computation.74 | convolution fusion | flops 5783073792 | bytes 19779936 | tf_op jit(solution)/shard_map/tf,df->td/dot_general | solution.py:205
  399.1 150.7 %while.27 = (s32[]{:T(128)}, bf16[6,1224,128]{1,2,0:T(8,128)(2,1)}, bf16[6,1224,128]{1,2,0:T(8,128)(2,1)}, bf16[6,1224,128]{1,2,0:T(8,128)(2,1)}, bf16[6,1224,12...) while((s32[]{:T(128)}, bf16[6,1224,128]{1,2,0:T(8,128)(2,1)}, ...), condition=%wide.region_12.13_spmd, body=%wide.region_10.12_spmd.sunk | while | flops 1945257856 | bytes 116307088 | solution.py:215
  414.6 4.9 convolution_multiply_fusion.7
  464.7 4.9 convolution_multiply_fusion.7
  549.9 10.0 %convolution_convert_fusion = bf16[768,2304]{1,0:T(8,128)(2,1)} fusion(bf16[1224,768]{1,0:T(8,128)(2,1)S(1)} %copy-done.1, f32[768]{0:T(1024)S(1)} %copy-done.33, f32[768]{0:T(1024)S(1)} %copy-done.20, f32[1224]{0:T(1024)S(1)} %copy-done.15, f32[1224]{0:T(1024)S(1)} %copy-done.9, bf16[1224,768]{0,1:T(8,128)(2,1)} %bitcast.184, ...), kind=kOutput, calls=%fused_computation.61 | convolution fusion | flops 4355997696 | bytes 11075136 | tf_op jit(solution)/shard_map/td,te->de/dot_general | solution.py:230
  560.0 12.1 %convolution_convert_fusion.2 = bf16[768,3072]{1,0:T(8,128)(2,1)} fusion(bf16[1224,3072]{1,0:T(8,128)(2,1)} %get-tuple-element.277, f32[1224,768]{1,0:T(8,128)} %copy-done.2, f32[768]{0:T(1024)S(1)} %copy-done.31, f32[768]{0:T(1024)S(1)} %copy-done.28, f32[1224]{0:T(1024)S(1)} %copy-done.26, f32[1224]{0:T(1024)S(1)} %copy-done.17), kind=kOutput, calls=%fused_computation.63 | convolution fusion | flops 5782616064 | bytes 16014912 | tf_op jit(solution)/shard_map/td,tf->df/dot_general | solution.py:204
  572.9 11.4 %convolution_convert_fusion.1 = bf16[3072,768]{1,0:T(8,128)(2,1)} fusion(bf16[1224,3072]{1,0:T(8,128)(2,1)} %get-tuple-element.251, bf16[1224,768]{1,0:T(8,128)(2,1)} %param.22, f32[1224]{0:T(1024)S(1)} %copy-done.22), kind=kOutput, calls=%fused_computation.62 | convolution fusion | flops 5780736000 | bytes 14123808 | tf_op jit(solution)/shard_map/tf,td->fd/dot_general | solution.py:200
  589.1 10.0 %fusion.44 = (bf16[768]{0:T(1024)(128)(2,1)S(1)}, f32[1224]{0:T(1024)S(1)}, f32[1224,768]{1,0:T(8,128)}) fusion(f32[768]{0:T(1024)S(1)} %copy-done.20, f32[1224]{0:T(1024)S(1)} %copy-done.9, bf16[1224,768]{1,0:T(8,128)(2,1)S(1)} %copy-done.1, bf16[768,2304]{1,0:T(8,128)(2,1)} %all-gather.8.cloned.1.call-done, bf16[1224,768]{0,1:T(8,128)(2,1)} %bitcast.185, ...), kind=kOutput, calls=%fused_computation.114 | convolution fusion | flops 4354226176 | bytes 14833728 | tf_op jit(solution)/shard_map/te,de->td/dot_general | solution.py:231
  599.1 25.7 %reduce-scatter.17.cloned.1.call-done = bf16[192,2304]{1,0:T(8,128)(2,1)} async-done(((bf16[768,2304]{1,0:T(8,128)(2,1)}), bf16[192,2304]{1,0:T(8,128)(2,1)}) %reduce-scatter.17.cloned.1.call-update) | async-done | bytes 884752 | tf_op jit(solution)/shard_map/reduce_scatter | solution.py:235
  633.5 79.2 %reduce-scatter.21.cloned.1.call-done = bf16[192,3072]{1,0:T(8,128)(2,1)} async-done(((bf16[768,3072]{1,0:T(8,128)(2,1)}), bf16[192,3072]{1,0:T(8,128)(2,1)}) %reduce-scatter.21.cloned.1.call-update) | async-done | bytes 1179664 | tf_op jit(solution)/shard_map/reduce_scatter | solution.py:241
  715.4 7.2 fusion.28
  722.7 19.6 %all-reduce.37 = (bf16[768]{0:T(1024)(128)(2,1)S(1)}, bf16[768]{0:T(1024)(128)(2,1)S(1)}, bf16[768]{0:T(1024)(128)(2,1)S(1)}, bf16[3072]{0:T(1024)(128)(2,1)S(1)...) all-reduce(bf16[768]{0:T(1024)(128)(2,1)S(1)} %get-tuple-element.26, ...), channel_id=10, replica_groups=mesh['gx'=4,'gy'=8] {'gx'}, use_global_device_ids=true, to_apply=%region_24.25.clone | all-reduce | flops 9216 | bytes 36864
  742.9 13.2 %all-reduce.35 = (bf16[192]{0:T(256)(128)(2,1)S(1)}, bf16[192]{0:T(256)(128)(2,1)S(1)}, bf16[192]{0:T(256)(128)(2,1)S(1)}, bf16[192]{0:T(256)(128)(2,1)S(1)}, bf...) all-reduce(bf16[192]{0:T(256)(128)(2,1)S(1)} %dynamic-update-slice., ...), channel_id=1, replica_groups=mesh['gx'=4,'gy'=8] {'gy'}, use_global_device_ids=true, to_apply=%add.15 | all-reduce | flops 2496 | bytes 9984
  756.4 10.7 %all-reduce.16 = bf16[768]{0:T(1024)(128)(2,1)S(1)} all-reduce(bf16[768]{0:T(1024)(128)(2,1)S(1)} %dynamic-update-slice.16), channel_id=1, replica_groups=mesh['gx'=4,'gy'=8] {'gx'}, use_global_device_ids=true, to_apply=%add.16 | all-reduce | flops 768 | bytes 3072
  772.4 29.6 %reduce-scatter.23.cloned.1.call-done = bf16[768,768]{1,0:T(8,128)(2,1)} async-done(((bf16[3072,768]{1,0:T(8,128)(2,1)}), bf16[768,768]{1,0:T(8,128)(2,1)}) %reduce-scatter.23.cloned.1.call-update) | async-done | bytes 1179664 | tf_op jit(solution)/shard_map/reduce_scatter | solution.py:244
  804.4 11.3 %fusion.30 = bf16[1224,768]{1,0:T(8,128)(2,1)} fusion(f32[1224,768]{1,0:T(8,128)} %copy-done.2, bf16[1224,3072]{1,0:T(8,128)(2,1)} %get-tuple-element.251, bf16[3072,768]{0,1:T(8,128)(2,1)} %all-gather.18.cloned.1.call-done, f32[768]{0:T(1024)S(1)} %convert_element_type.210), kind=kOutput, calls=%fused_computation.83 | convolution fusion | flops 5778376704 | bytes 17882112 | tf_op jit(solution)/shard_map/dot_general | solution.py:174
  815.7 23.8 %reduce-scatter.27.cloned.1.call-done = bf16[96,192]{1,0:T(8,128)(2,1)} async-done(((bf16[768,192]{1,0:T(8,128)(2,1)}), bf16[96,192]{1,0:T(8,128)(2,1)}) %reduce-scatter.27.cloned.1.call-update) | async-done | bytes 36880
  841.1 38.3 %reduce-scatter.25.cloned.1.call-done = bf16[288,192]{1,0:T(8,128)(2,1)} async-done(((bf16[2304,192]{1,0:T(8,128)(2,1)}), bf16[288,192]{1,0:T(8,128)(2,1)}) %reduce-scatter.25.cloned.1.call-update) | async-done | bytes 110608
  881.1 40.4 %reduce-scatter.29.cloned.1.call-done = bf16[384,192]{1,0:T(8,128)(2,1)} async-done(((bf16[3072,192]{1,0:T(8,128)(2,1)}), bf16[384,192]{1,0:T(8,128)(2,1)}) %reduce-scatter.29.cloned.1.call-update) | async-done | bytes 147472
  923.3 38.4 %reduce-scatter.31.cloned.1.call-done = bf16[96,768]{1,0:T(8,128)(2,1)} async-done(((bf16[768,768]{1,0:T(8,128)(2,1)}), bf16[96,768]{1,0:T(8,128)(2,1)}) %reduce-scatter.31.cloned.1.call-update) | async-done | bytes 147472
  (415 shorter events, 291.2 us)
Async XLA Ops:
  7.2 30.1 %all-gather.12.cloned.1.call-start = ((), (), s32[]{:S(2)}) async-start(), calls=%async_computation.10 | async-start | bytes 1327104 | tf_op jit(solution)/shard_map/all_gather | solution.py:117
  8.0 84.7 %all-gather.16.cloned.1.call-start = ((), (), s32[]{:S(2)}) async-start(), calls=%async_computation.12 | async-start | bytes 1327104 | tf_op jit(solution)/shard_map/all_gather | solution.py:118
  8.8 82.3 %copy-start = (bf16[1224,768]{1,0:T(8,128)(2,1)S(1)}, bf16[1224,768]{1,0:T(8,128)(2,1)}, u32[]{:S(2)}) copy-start(bf16[1224,768]{1,0:T(8,128)(2,1)} %param.20) | copy-start | bytes 5640196
  8.8 127.3 %all-gather.8.cloned.1.call-start = ((), (), s32[]{:S(2)}) async-start(), calls=%async_computation.8 | async-start | bytes 4423680 | tf_op jit(solution)/shard_map/all_gather | solution.py:130
  24.4 201.0 %all-gather.10.cloned.1.call-start = ((), (), s32[]{:S(2)}) async-start(), calls=%async_computation.9 | async-start | bytes 1474560 | tf_op jit(solution)/shard_map/all_gather | solution.py:131
  35.9 221.3 %all-gather.14.cloned.1.call-start = ((), (), s32[]{:S(2)}) async-start(), calls=%async_computation.11 | async-start | bytes 5898240 | tf_op jit(solution)/shard_map/all_gather | solution.py:132
  37.4 309.1 %all-gather.18.cloned.1.call-start = ((), (), s32[]{:S(2)}) async-start(), calls=%async_computation.13 | async-start | bytes 5898240 | tf_op jit(solution)/shard_map/all_gather | solution.py:133
  76.1 67.4 %copy-start.19 = (f32[768]{0:T(1024)}, f32[768]{0:T(1024)S(1)}, u32[]{:S(2)}) copy-start(f32[768]{0:T(1024)S(1)} %convert_element_type.194) | copy-start | bytes 9220
  76.1 67.4 %copy-start.32 = (f32[768]{0:T(1024)}, f32[768]{0:T(1024)S(1)}, u32[]{:S(2)}) copy-start(f32[768]{0:T(1024)S(1)} %convert_element_type.195) | copy-start | bytes 9220
  76.8 302.4 %copy-start.27 = (f32[768]{0:T(1024)}, f32[768]{0:T(1024)S(1)}, u32[]{:S(2)}) copy-start(f32[768]{0:T(1024)S(1)} %convert_element_type.205) | copy-start | bytes 9220
  76.8 180.4 %copy-start.30 = (f32[768]{0:T(1024)}, f32[768]{0:T(1024)S(1)}, u32[]{:S(2)}) copy-start(f32[768]{0:T(1024)S(1)} %convert_element_type.206) | copy-start | bytes 9220
  91.4 52.1 %copy-start.8 = (f32[1224]{0:T(1024)}, f32[1224]{0:T(1024)S(1)}, u32[]{:S(2)}) copy-start(f32[1224]{0:T(1024)S(1)} %broadcast_multiply_fusion.1) | copy-start | bytes 14692
  92.7 50.8 %copy-start.14 = (f32[1224]{0:T(1024)}, f32[1224]{0:T(1024)S(1)}, u32[]{:S(2)}) copy-start(f32[1224]{0:T(1024)S(1)} %fusion.36) | copy-start | bytes 14692
  92.7 494.4 %reduce-scatter.19.cloned.1.call-start = ((), (), s32[]{:S(2)}) async-start(), calls=%async_computation.15 | async-start | bytes 1474560 | tf_op jit(solution)/shard_map/reduce_scatter | solution.py:238
  229.2 149.9 %copy-start.16 = (f32[1224]{0:T(1024)}, f32[1224]{0:T(1024)S(1)}, u32[]{:S(2)}) copy-start(f32[1224]{0:T(1024)S(1)} %broadcast_multiply_fusion) | copy-start | bytes 14692
  231.6 147.6 %copy-start.25 = (f32[1224]{0:T(1024)}, f32[1224]{0:T(1024)S(1)}, u32[]{:S(2)}) copy-start(f32[1224]{0:T(1024)S(1)} %fusion.37) | copy-start | bytes 14692
  257.2 89.3 %copy-start.7 = (bf16[1224,768]{1,0:T(8,128)(2,1)S(1)}, bf16[1224,768]{1,0:T(8,128)(2,1)}, u32[]{:S(2)}) copy-start(bf16[1224,768]{1,0:T(8,128)(2,1)} %param.22) | copy-start | bytes 5640196
  257.2 89.3 %copy-start.21 = (f32[1224]{0:T(1024)S(1)}, f32[1224]{0:T(1024)}, u32[]{:S(2)}) copy-start(f32[1224]{0:T(1024)} %fusion.35) | copy-start | bytes 14692
  387.6 237.2 %reduce-scatter.17.cloned.1.call-start = ((), (), s32[]{:S(2)}) async-start(), calls=%async_computation.14 | async-start | bytes 4423680 | tf_op jit(solution)/shard_map/reduce_scatter | solution.py:235
  399.0 150.8 %copy-start.1 = (bf16[1224,768]{1,0:T(8,128)(2,1)S(1)}, bf16[1224,768]{1,0:T(8,128)(2,1)}, u32[]{:S(2)}) copy-start(bf16[1224,768]{1,0:T(8,128)(2,1)} %param.20) | copy-start | bytes 5640196
  399.0 150.8 %copy-start.9 = (f32[1224]{0:T(1024)S(1)}, f32[1224]{0:T(1024)}, u32[]{:S(2)}) copy-start(f32[1224]{0:T(1024)} %copy-done.8) | copy-start | bytes 14692
  399.0 150.8 %copy-start.15 = (f32[1224]{0:T(1024)S(1)}, f32[1224]{0:T(1024)}, u32[]{:S(2)}) copy-start(f32[1224]{0:T(1024)} %copy-done.14) | copy-start | bytes 14692
  399.0 150.8 %copy-start.20 = (f32[768]{0:T(1024)S(1)}, f32[768]{0:T(1024)}, u32[]{:S(2)}) copy-start(f32[768]{0:T(1024)} %copy-done.19) | copy-start | bytes 9220
  399.1 150.8 %copy-start.33 = (f32[768]{0:T(1024)S(1)}, f32[768]{0:T(1024)}, u32[]{:S(2)}) copy-start(f32[768]{0:T(1024)} %copy-done.32) | copy-start | bytes 9220
  560.0 152.8 %reduce-scatter.21.cloned.1.call-start = ((), (), s32[]{:S(2)}) async-start(), calls=%async_computation.16 | async-start | bytes 5898240 | tf_op jit(solution)/shard_map/reduce_scatter | solution.py:241
  572.2 229.8 %reduce-scatter.23.cloned.1.call-start = ((), (), s32[]{:S(2)}) async-start(), calls=%async_computation.17 | async-start | bytes 5898240 | tf_op jit(solution)/shard_map/reduce_scatter | solution.py:244
  584.3 255.3 %reduce-scatter.27.cloned.1.call-start = ((), (), s32[]{:S(2)}) async-start(), calls=%async_computation.19 | async-start | bytes 442368
  589.1 38.2 %copy-start.13 = (f32[1224]{0:T(1024)S(1)}, f32[1224]{0:T(1024)}, u32[]{:S(2)}) copy-start(f32[1224]{0:T(1024)} %copy-done.12) | copy-start | bytes 14692
  589.1 290.3 %reduce-scatter.25.cloned.1.call-start = ((), (), s32[]{:S(2)}) async-start(), calls=%async_computation.18 | async-start | bytes 1327104
  627.2 294.3 %reduce-scatter.29.cloned.1.call-start = ((), (), s32[]{:S(2)}) async-start(), calls=%async_computation.20 | async-start | bytes 1769472
  631.0 84.4 %copy-start.24 = (f32[1224]{0:T(1024)S(1)}, f32[1224]{0:T(1024)}, u32[]{:S(2)}) copy-start(f32[1224]{0:T(1024)} %copy-done.23) | copy-start | bytes 14692
  715.3 246.4 %reduce-scatter.31.cloned.1.call-start = ((), (), s32[]{:S(2)}) async-start(), calls=%async_computation.21 | async-start | bytes 1327104
  (44 other events, 546.7 us)
Sparse Core Ops, SparseCore 0:
  9.9 27.3 all-gather.11
  39.2 24.6 all-gather.15
  66.0 70.0 all-gather.7
  138.1 29.0 all-gather.9
  168.6 88.5 all-gather.13
  258.6 87.8 all-gather.17
  387.8 27.5 reduce-scatter.18
  560.1 64.7 reduce-scatter.16
  627.2 85.5 reduce-scatter.20
  714.9 87.0 reduce-scatter.22
  805.1 34.3 reduce-scatter.26
  842.6 36.7 reduce-scatter.24
  883.0 38.4 reduce-scatter.28
  924.9 36.7 reduce-scatter.30
where the time goes:
time: 979 us; the launch traced here: 971 us
  waiting for transfers between devices  394 us (40%)
  matrix products  259 us (26%)
  local copies, waits for them, and re-layouts  113 us (12%)
  blocking collectives  113 us (12%)
  other arithmetic  69.5 us (7%)
  between operations  20.5 us (2%)
    unnamed x18, waiting for transfers between devices  142 us
    reduce_scatter x1, waiting for transfers between devices, per_device(): lax.psum_scatter(grad_w_up.astype(jnp.bfloat16), 'gx', scatter_dimension=...  79.2 us
    unnamed x5, blocking collectives  76.1 us
    all_gather x1, waiting for transfers between devices, per_device(): lax.all_gather(by_cols[3], 'gx', axis=0, tiled=True)  46.9 us
    dynamic_slice x48, local copies, waits for them, and re-layouts, per_device(): lax.map(attend, (query_blocks, key_blocks, value_blocks, pair_lengths))  43.8 us
    all_gather x1, waiting for transfers between devices, per_device(): lax.all_gather(by_cols[0], 'gx', axis=0, tiled=True)  43.1 us
    dot_general x1, matrix products, per_device(): jnp.dot(normed_two_low, mat_up, preferred_element_type=jnp.float32) + vec_up  42.4 us
    dot_general x12, matrix products, block_scores(): jnp.einsum('qhd,khd->hqk', query_heads, key_heads, preferred_element_type...  35.3 us
  transfers between devices with their start and end apart: 14, of which 11 were waited for; matrix products, arithmetic and copies ran while one was open for 41% of the time, Pallas kernels for 0%

commit v1 on v0

--- a/solution.py
+++ b/solution.py
@@ -7,6 +7,22 @@
 HEAD_DIM = 64
 EPSILON = 1e-06
 NEG_FILL = -1e30
+
+
+def desk_produce(xin):
+    axis_total = lax.psum(1, axis_name="gx")
+    blocks_here = [(dd, (dd + 1) % axis_total) for dd in range(axis_total)]
+    grid = [(dd, (dd - 1) % axis_total) for dd in range(axis_total)]
+    main, prior = ([xin], [xin])
+    for _ in range(axis_total // 2):
+        z2 = lax.ppermute(main[-1], axis_name="gx", perm=blocks_here)
+        main.append(z2)
+    for _ in range((axis_total - 1) // 2):
+        z_new = lax.ppermute(prior[-1], axis_name="gx", perm=grid)
+        prior.append(z_new)
+    local_now = jnp.concatenate([*main[::-1], *prior[1:]], 0)
+    carry_out = lax.axis_index("gx")
+    return jnp.roll(local_now, (carry_out - axis_total // 2) * xin.shape[0], 0)
 
 
 def layer_norm(values, gain_vec, shift_vec):
@@ -127,7 +143,7 @@
         lax.all_gather(shift_two, "gy", axis=0, tiled=True),
     )
     gathered = (
-        lax.all_gather(by_cols[0], "gx", axis=0, tiled=True),
+        desk_produce(by_cols[0]),
         lax.all_gather(by_cols[1], "gx", axis=0, tiled=True),
         lax.all_gather(by_cols[2], "gx", axis=0, tiled=True),
         lax.all_gather(by_cols[3], "gx", axis=0, tiled=True),

time: 979 us -> 993 us (1.014)
  waiting for transfers between devices: 394 us -> 345 us
  blocking collectives: 113 us -> 144 us
  local copies, waits for them, and re-layouts: 113 us -> 131 us
    all_gather x1, waiting for transfers between devices: 43.1 us -> 0.02 us  [per_device(): lax.all_gather(regather_cols[0], 'gx', axis=0, tiled=True)]
    unnamed x5, blocking collectives: 76.1 us -> 106 us
    all_gather x1, waiting for transfers between devices: 25.5 us -> 10.3 us  [per_device(): lax.all_gather(by_cols[2], 'gx', axis=0, tiled=True)]
    concatenate x0 -> x1, local copies, waits for them, and re-layouts: none -> 13 us  [desk_produce(): return jnp.roll(local_now, (carry_out - axis_total // 2) * xin.shape[0], 0)]
    ppermute x0 -> x3, waiting for transfers between devices: none -> 10.8 us  [the longest x2 10.8 us: desk_produce(): z2 = lax.ppermute(main[-1], axis_name='gx', perm=blocks_here)]
    unnamed x156 -> x148, local copies, waits for them, and re-layouts: 25.6 us -> 23.2 us
  transfers between devices with their start and end apart: 14 -> 17, of which waited for: 11 -> 10; matrix products, arithmetic and copies ran while one was open for 41% -> 43% of each run, Pallas kernels for 0% -> 0%
where the time goes in v1:
time: 993 us; the launch traced here: 985 us
  waiting for transfers between devices  345 us (35%)
  matrix products  263 us (26%)
  blocking collectives  144 us (15%)
  local copies, waits for them, and re-layouts  131 us (13%)
  other arithmetic  75 us (8%)
  between operations  20.2 us (2%)
    unnamed x18, waiting for transfers between devices  142 us
    unnamed x5, blocking collectives  106 us
    reduce_scatter x1, waiting for transfers between devices, per_device(): lax.psum_scatter(grad_w_up.astype(jnp.bfloat16), 'gx', scatter_dimension=...  79.2 us
    all_gather x1, waiting for transfers between devices, per_device(): lax.all_gather(by_cols[3], 'gx', axis=0, tiled=True)  47.1 us
    dynamic_slice x48, local copies, waits for them, and re-layouts, per_device(): lax.map(attend, (query_blocks, key_blocks, value_blocks, pair_lengths))  43.8 us
    dot_general x1, matrix products, per_device(): jnp.dot(normed_two_low, mat_up, preferred_element_type=jnp.float32) + vec_up  42.2 us
    dot_general x12, matrix products, block_scores(): jnp.einsum('qhd,khd->hqk', query_heads, key_heads, preferred_element_type...  36.5 us
    reduce_scatter x1, waiting for transfers between devices, per_device(): lax.psum_scatter(grad_w_down.astype(jnp.bfloat16), 'gx', scatter_dimensio...  29.7 us
  transfers between devices with their start and end apart: 17, of which 10 were waited for; matrix products, arithmetic and copies ran while one was open for 43% of the time, Pallas kernels for 0%

profile of v1, /device:TPU:0, one launch (start us, length us, event | category | flops | bytes accessed | tf_op | source)
XLA Modules:
  0.0 984.8 jit_solution(18060099618871704560)
XLA Ops:
  9.0 11.0 %all_gather.94 = bf16[192,768]{0,1:T(8,128)(2,1)S(1)} all-gather(bf16[192,96]{0,1:T(8,128)(2,1)S(1)} %copy.76), channel_id=1, replica_groups=mesh['gx'=4,'gy'=8] {'gy'}, dimensions={1}, use_global_device_ids=true | all-gather | bytes 331776 | tf_op jit(solution)/shard_map/all_gather | solution.py:132
  22.0 13.6 %all_gather.89 = bf16[192,2304]{0,1:T(8,128)(2,1)S(1)} all-gather(bf16[192,288]{0,1:T(8,128)(2,1)S(1)} %copy.64), channel_id=1, replica_groups=mesh['gx'=4,'gy'=8] {'gy'}, dimensions={1}, use_global_device_ids=true | all-gather | bytes 995328 | tf_op jit(solution)/shard_map/all_gather | solution.py:131
  45.8 14.0 %all-reduce.36 = (bf16[768]{0:T(1024)(128)(2,1)S(1)}, bf16[192]{0:T(256)(128)(2,1)S(1)}, bf16[192]{0:T(256)(128)(2,1)S(1)}, bf16[192]{0:T(256)(128)(2,1)S(1)}, b...) all-reduce(bf16[768]{0:T(1024)(128)(2,1)S(1)} %dynamic-update-slice, ...), channel_id=1, replica_groups=mesh['gx'=4,'gy'=8] {'gy'}, use_global_device_ids=true, to_apply=%add.14 | all-reduce | flops 2112 | bytes 8448
  61.3 48.7 %all-reduce.38 = (bf16[768]{0:T(1024)(128)(2,1)S(1)}, bf16[768]{0:T(1024)(128)(2,1)S(1)}, bf16[768]{0:T(1024)(128)(2,1)S(1)}, bf16[768]{0:T(1024)(128)(2,1)S(1)}...) all-reduce(bf16[768]{0:T(1024)(128)(2,1)S(1)} %dynamic-update-slice, ...), channel_id=1, replica_groups=mesh['gx'=4,'gy'=8] {'gx'}, use_global_device_ids=true, to_apply=%add.7 | all-reduce | flops 5376 | bytes 21504
  110.8 13.1 %all-gather = bf16[4,1,768]{2,1,0:T(2,128)(2,1)S(1)} all-gather(bf16[1,1,768]{2,1,0:T(2,128)(2,1)S(1)} %reshape.302), channel_id=1, replica_groups=mesh['gx'=4,'gy'=8] {'gx'}, dimensions={0}, use_global_device_ids=true | all-gather | bytes 7680 | tf_op jit(solution)/shard_map/all_gather | solution.py:153
  131.4 10.8 %collective-permute-done.1 = bf16[192,2304]{1,0:T(8,128)(2,1)} collective-permute-done((bf16[192,2304]{1,0:T(8,128)(2,1)}, bf16[192,2304]{1,0:T(8,128)(2,1)}, u32[]{:S(2)}, u32[]{:S(2)}) %collective-permute-start.1) | collective-permute-done | bytes 884768 | tf_op jit(solution)/shard_map/ppermute | solution.py:18
  144.6 13.0 %concatenate.13 = bf16[1536,2304]{0,1:T(8,128)(2,1)} concatenate(bf16[192,2304]{0,1:T(8,128)(2,1)} %copy.67, bf16[192,2304]{0,1:T(8,128)(2,1)} %copy.68, bf16[192,2304]{0,1:T(8,128)(2,1)S(1)} %all_gather.89, bf16[192,2304]{0,1:T(8,128)(2,1)} %copy.69, bf16[192,2304]{0,1:T(8,128)(2,1)} %copy.67, bf16[192,2304]{0,1:T(8,128)(2,1)} %copy.68, bf16[192,2304]{0,1:T(8,128)(2,1)S(1)} %all_gather.89, ...), dimensions={0} | concatenate | bytes 14155776 | tf_op jit(solution)/shard_map/jit(_roll_dynamic)/concatenate | solution.py:25
  157.6 7.9 fusion.14
  181.7 65.9 %while.26 = (s32[]{:T(128)}, bf16[6,1224,128]{1,2,0:T(8,128)(2,1)}, f32[6,2,1224]{2,1,0:T(2,128)}, bf16[6,1224,128]{1,2,0:T(8,128)(2,1)}, s32[6]{0:T(128)S(1)}, ...) while((s32[]{:T(128)}, bf16[6,1224,128]{1,2,0:T(8,128)(2,1)}, ...), condition=%wide.region_5.6_spmd, body=%wide.region_2.5_spmd.sunk | while | flops 791035712 | bytes 39813052 | solution.py:179
  256.6 10.3 %all-gather.12.cloned.1.call-done = bf16[768,3072]{1,0:T(8,128)(2,1)} async-done(((bf16[192,3072]{1,0:T(8,128)(2,1)}), bf16[768,3072]{1,0:T(8,128)(2,1)}) %all-gather.12.cloned.1.call-update) | async-done | bytes 4718608 | tf_op jit(solution)/shard_map/all_gather | solution.py:148
  266.9 42.2 %multiply_convert_fusion.1 = (bf16[1224,3072]{1,0:T(8,128)(2,1)}, f32[1224,3072]{1,0:T(8,128)}, f32[1224,3072]{1,0:T(8,128)}) fusion(f32[3072]{0:T(1024)S(1)} %bitcast.195, bf16[768,3072]{1,0:T(8,128)(2,1)} %all-gather.12.cloned.1.call-done, f32[1224,768]{1,0:T(8,128)} %get-tuple-element.272, f32[768]{0:T(1024)S(1)} %convert_element_type.206, ...), kind=kOutput, calls=%fused_computation.34 | convolution fusion | flops 6028425216 | bytes 46108224 | tf_op jit(solution)/shard_map/dot_general | solution.py:186
  309.1 47.1 %all-gather.16.cloned.1.call-done = bf16[3072,768]{0,1:T(8,128)(2,1)} async-done(((bf16[768,768]{0,1:T(8,128)(2,1)}), bf16[3072,768]{0,1:T(8,128)(2,1)}) %all-gather.16.cloned.1.call-update) | async-done | bytes 4718608 | tf_op jit(solution)/shard_map/all_gather | solution.py:149
  356.2 19.9 %fusion.55 = (bf16[3072]{0:T(1024)(128)(2,1)}, bf16[1224,3072]{1,0:T(8,128)(2,1)}) fusion(f32[1224,3072]{1,0:T(8,128)} %get-tuple-element.252, f32[1224,3072]{1,0:T(8,128)} %get-tuple-element.273, bf16[3072,768]{0,1:T(8,128)(2,1)} %all-gather.16.cloned.1.call-done, bf16[1224,768]{1,0:T(8,128)(2,1)S(1)} %copy-done.4, f32[1224]{0:T(1024)S(1)} %copy-done.17), kind=kOutput, calls=%fused_computation.124 | convolution fusion | flops 5834775552 | bytes 44210976 | tf_op jit(solution)/shard_map/td,fd->tf/dot_general | solution.py:217
  376.1 12.4 %multiply_reduce_fusion.1 = (bf16[768]{0:T(1024)(128)(2,1)}, f32[1224]{0:T(1024)S(1)}, bf16[768]{0:T(1024)(128)(2,1)}, f32[1224,768]{1,0:T(8,128)S(1)}) fusion(f32[1224,768]{1,0:T(8,128)} %get-tuple-element.272, f32[1224]{0:T(1024)S(1)} %fusion.38, f32[1224]{0:T(1024)S(1)} %broadcast_multiply_fusion, f32[768]{0:T(1024)S(1)} %convert_element_type.205, ...), kind=kOutput, calls=%fused_computation.74 | convolution fusion | flops 5783073792 | bytes 19779936 | tf_op jit(solution)/shard_map/tf,df->td/dot_general | solution.py:221
  393.0 5.8 convolution_convert_fusion.4
  411.3 152.6 %while.27 = (s32[]{:T(128)}, bf16[6,1224,128]{1,2,0:T(8,128)(2,1)}, bf16[6,1224,128]{1,2,0:T(8,128)(2,1)}, bf16[6,1224,128]{1,2,0:T(8,128)(2,1)}, bf16[6,1224,12...) while((s32[]{:T(128)}, bf16[6,1224,128]{1,2,0:T(8,128)(2,1)}, ...), condition=%wide.region_12.13_spmd, body=%wide.region_10.12_spmd.sunk | while | flops 1945257856 | bytes 116307088 | solution.py:231
  564.0 10.1 %convolution_convert_fusion = bf16[768,2304]{1,0:T(8,128)(2,1)} fusion(bf16[1224,768]{1,0:T(8,128)(2,1)S(1)} %copy-done.1, f32[768]{0:T(1024)S(1)} %copy-done.27, f32[768]{0:T(1024)S(1)} %copy-done.16, f32[1224]{0:T(1024)S(1)} %copy-done.12, f32[1224]{0:T(1024)S(1)} %copy-done.6, bf16[1224,768]{0,1:T(8,128)(2,1)} %bitcast.183, ...), kind=kOutput, calls=%fused_computation.61 | convolution fusion | flops 4355997696 | bytes 11075136 | tf_op jit(solution)/shard_map/td,te->de/dot_general | solution.py:246
  574.3 12.1 %convolution_convert_fusion.2 = bf16[768,3072]{1,0:T(8,128)(2,1)} fusion(bf16[1224,3072]{1,0:T(8,128)(2,1)} %get-tuple-element.277, f32[1224,768]{1,0:T(8,128)} %get-tuple-element.272, f32[768]{0:T(1024)S(1)} %copy-done.29, f32[768]{0:T(1024)S(1)} %copy-done.24, f32[1224]{0:T(1024)S(1)} %copy-done.22, f32[1224]{0:T(1024)S(1)} %copy-done.14), kind=kOutput, calls=%fused_computation.63 | convolution fusion | flops 5782616064 | bytes 16014912 | tf_op jit(solution)/shard_map/td,tf->df/dot_general | solution.py:220
  587.1 11.3 %convolution_convert_fusion.1 = bf16[3072,768]{1,0:T(8,128)(2,1)} fusion(bf16[1224,3072]{1,0:T(8,128)(2,1)} %get-tuple-element.251, bf16[1224,768]{1,0:T(8,128)(2,1)} %param.22, f32[1224]{0:T(1024)S(1)} %copy-done.18), kind=kOutput, calls=%fused_computation.62 | convolution fusion | flops 5780736000 | bytes 14123808 | tf_op jit(solution)/shard_map/tf,td->fd/dot_general | solution.py:216
  603.3 10.1 %fusion.46 = (bf16[768]{0:T(1024)(128)(2,1)S(1)}, f32[1224]{0:T(1024)S(1)}, f32[1224,768]{1,0:T(8,128)}) fusion(f32[768]{0:T(1024)S(1)} %copy-done.16, f32[1224]{0:T(1024)S(1)} %copy-done.6, bf16[1224,768]{1,0:T(8,128)(2,1)S(1)} %copy-done.1, bf16[768,2304]{1,0:T(8,128)(2,1)} %all-gather.18.cloned.1.call-done, bf16[1224,768]{0,1:T(8,128)(2,1)} %bitcast.184, ...), kind=kOutput, calls=%fused_computation.116 | convolution fusion | flops 4354226176 | bytes 14833728 | tf_op jit(solution)/shard_map/te,de->td/dot_general | solution.py:247
  613.5 25.7 %reduce-scatter.17.cloned.1.call-done = bf16[192,2304]{1,0:T(8,128)(2,1)} async-done(((bf16[768,2304]{1,0:T(8,128)(2,1)}), bf16[192,2304]{1,0:T(8,128)(2,1)}) %reduce-scatter.17.cloned.1.call-update) | async-done | bytes 884752 | tf_op jit(solution)/shard_map/reduce_scatter | solution.py:251
  647.9 79.2 %reduce-scatter.21.cloned.1.call-done = bf16[192,3072]{1,0:T(8,128)(2,1)} async-done(((bf16[768,3072]{1,0:T(8,128)(2,1)}), bf16[192,3072]{1,0:T(8,128)(2,1)}) %reduce-scatter.21.cloned.1.call-update) | async-done | bytes 1179664 | tf_op jit(solution)/shard_map/reduce_scatter | solution.py:257
  729.7 7.2 fusion.28
  737.0 19.6 %all-reduce.37 = (bf16[768]{0:T(1024)(128)(2,1)S(1)}, bf16[768]{0:T(1024)(128)(2,1)S(1)}, bf16[768]{0:T(1024)(128)(2,1)S(1)}, bf16[3072]{0:T(1024)(128)(2,1)S(1)...) all-reduce(bf16[768]{0:T(1024)(128)(2,1)S(1)} %get-tuple-element.26, ...), channel_id=10, replica_groups=mesh['gx'=4,'gy'=8] {'gx'}, use_global_device_ids=true, to_apply=%region_24.25.clone | all-reduce | flops 9216 | bytes 36864
  757.3 13.2 %all-reduce.35 = (bf16[192]{0:T(256)(128)(2,1)S(1)}, bf16[192]{0:T(256)(128)(2,1)S(1)}, bf16[192]{0:T(256)(128)(2,1)S(1)}, bf16[192]{0:T(256)(128)(2,1)S(1)}, bf...) all-reduce(bf16[192]{0:T(256)(128)(2,1)S(1)} %dynamic-update-slice., ...), channel_id=1, replica_groups=mesh['gx'=4,'gy'=8] {'gy'}, use_global_device_ids=true, to_apply=%add.15 | all-reduce | flops 2496 | bytes 9984
  770.7 10.7 %all-reduce.16 = bf16[768]{0:T(1024)(128)(2,1)S(1)} all-reduce(bf16[768]{0:T(1024)(128)(2,1)S(1)} %dynamic-update-slice.16), channel_id=1, replica_groups=mesh['gx'=4,'gy'=8] {'gx'}, use_global_device_ids=true, to_apply=%add.16 | all-reduce | flops 768 | bytes 3072
  786.7 29.7 %reduce-scatter.23.cloned.1.call-done = bf16[768,768]{1,0:T(8,128)(2,1)} async-done(((bf16[3072,768]{1,0:T(8,128)(2,1)}), bf16[768,768]{1,0:T(8,128)(2,1)}) %reduce-scatter.23.cloned.1.call-update) | async-done | bytes 1179664 | tf_op jit(solution)/shard_map/reduce_scatter | solution.py:260
  818.8 11.3 %fusion.31 = bf16[1224,768]{1,0:T(8,128)(2,1)} fusion(f32[1224,768]{1,0:T(8,128)} %get-tuple-element.272, bf16[1224,3072]{1,0:T(8,128)(2,1)} %get-tuple-element.251, bf16[3072,768]{0,1:T(8,128)(2,1)} %all-gather.16.cloned.1.call-done, f32[768]{0:T(1024)S(1)} %convert_element_type.210), kind=kOutput, calls=%fused_computation.84 | convolution fusion | flops 5778376704 | bytes 17882112 | tf_op jit(solution)/shard_map/dot_general | solution.py:190
  830.1 23.7 %reduce-scatter.27.cloned.1.call-done = bf16[96,192]{1,0:T(8,128)(2,1)} async-done(((bf16[768,192]{1,0:T(8,128)(2,1)}), bf16[96,192]{1,0:T(8,128)(2,1)}) %reduce-scatter.27.cloned.1.call-update) | async-done | bytes 36880
  855.4 38.3 %reduce-scatter.25.cloned.1.call-done = bf16[288,192]{1,0:T(8,128)(2,1)} async-done(((bf16[2304,192]{1,0:T(8,128)(2,1)}), bf16[288,192]{1,0:T(8,128)(2,1)}) %reduce-scatter.25.cloned.1.call-update) | async-done | bytes 110608
  895.5 40.3 %reduce-scatter.29.cloned.1.call-done = bf16[384,192]{1,0:T(8,128)(2,1)} async-done(((bf16[3072,192]{1,0:T(8,128)(2,1)}), bf16[384,192]{1,0:T(8,128)(2,1)}) %reduce-scatter.29.cloned.1.call-update) | async-done | bytes 147472
  937.6 38.4 %reduce-scatter.31.cloned.1.call-done = bf16[96,768]{1,0:T(8,128)(2,1)} async-done(((bf16[768,768]{1,0:T(8,128)(2,1)}), bf16[96,768]{1,0:T(8,128)(2,1)}) %reduce-scatter.31.cloned.1.call-update) | async-done | bytes 147472
  (417 shorter events, 313.0 us)
Async XLA Ops:
  7.3 117.8 %copy-start = (bf16[1224,768]{1,0:T(8,128)(2,1)S(1)}, bf16[1224,768]{1,0:T(8,128)(2,1)}, u32[]{:S(2)}) copy-start(bf16[1224,768]{1,0:T(8,128)(2,1)} %param.20) | copy-start | bytes 5640196
  7.3 172.8 %all-gather.10.cloned.1.call-start = ((), (), s32[]{:S(2)}) async-start(), calls=%async_computation.9 | async-start | bytes 1327104 | tf_op jit(solution)/shard_map/all_gather | solution.py:133
  8.0 239.6 %all-gather.8.cloned.1.call-start = ((), (), s32[]{:S(2)}) async-start(), calls=%async_computation.8 | async-start | bytes 1474560 | tf_op jit(solution)/shard_map/all_gather | solution.py:147
  20.9 235.4 %all-gather.14.cloned.1.call-start = ((), (), s32[]{:S(2)}) async-start(), calls=%async_computation.11 | async-start | bytes 1327104 | tf_op jit(solution)/shard_map/all_gather | solution.py:134
  36.9 87.6 %collective-permute-start = (bf16[192,2304]{1,0:T(8,128)(2,1)}, bf16[192,2304]{1,0:T(8,128)(2,1)}, u32[]{:S(2)}, u32[]{:S(2)}) collective-permute-start(bf16[192,2304]{1,0:T(8,128)(2,1)} %copy.65), channel_id=1, source_target_pairs={{0,8},{8,16},{16,24},{24,0},{1,9},{9,17},{17,25},{25,1},{2,10},{10... | collective-permute-start | bytes 2654216 | tf_op jit(solution)/shard_map/ppermute | solution.py:18
  38.7 90.4 %collective-permute-start.2 = (bf16[192,2304]{1,0:T(8,128)(2,1)}, bf16[192,2304]{1,0:T(8,128)(2,1)}, u32[]{:S(2)}, u32[]{:S(2)}) collective-permute-start(bf16[192,2304]{1,0:T(8,128)(2,1)} %copy.65), channel_id=1, source_target_pairs={{0,24},{8,0},{16,8},{24,16},{1,25},{9,1},{17,9},{25,17},{2,26},{10... | collective-permute-start | bytes 2654216 | tf_op jit(solution)/shard_map/ppermute | solution.py:21
  41.1 225.8 %all-gather.12.cloned.1.call-start = ((), (), s32[]{:S(2)}) async-start(), calls=%async_computation.10 | async-start | bytes 5898240 | tf_op jit(solution)/shard_map/all_gather | solution.py:148
  110.0 47.5 %copy-start.15 = (f32[768]{0:T(1024)}, f32[768]{0:T(1024)S(1)}, u32[]{:S(2)}) copy-start(f32[768]{0:T(1024)S(1)} %convert_element_type.194) | copy-start | bytes 9220
  110.0 47.5 %copy-start.26 = (f32[768]{0:T(1024)}, f32[768]{0:T(1024)S(1)}, u32[]{:S(2)}) copy-start(f32[768]{0:T(1024)S(1)} %convert_element_type.195) | copy-start | bytes 9220
  110.7 277.8 %copy-start.23 = (f32[768]{0:T(1024)}, f32[768]{0:T(1024)S(1)}, u32[]{:S(2)}) copy-start(f32[768]{0:T(1024)S(1)} %convert_element_type.205) | copy-start | bytes 9220
  110.8 156.2 %copy-start.28 = (f32[768]{0:T(1024)}, f32[768]{0:T(1024)S(1)}, u32[]{:S(2)}) copy-start(f32[768]{0:T(1024)S(1)} %convert_element_type.206) | copy-start | bytes 9220
  124.5 17.7 %collective-permute-start.1 = (bf16[192,2304]{1,0:T(8,128)(2,1)}, bf16[192,2304]{1,0:T(8,128)(2,1)}, u32[]{:S(2)}, u32[]{:S(2)}) collective-permute-start(bf16[192,2304]{1,0:T(8,128)(2,1)} %collective-permute-done), channel_id=1, source_target_pairs={{0,8},{8,16},{16,24},{24,0},{1,9},{9,17},{17,25},{25,1},{2,10},{10... | collective-permute-start | bytes 2654216 | tf_op jit(solution)/shard_map/ppermute | solution.py:18
  180.1 176.1 %all-gather.16.cloned.1.call-start = ((), (), s32[]{:S(2)}) async-start(), calls=%async_computation.12 | async-start | bytes 5898240 | tf_op jit(solution)/shard_map/all_gather | solution.py:149
  253.1 135.4 %copy-start.13 = (f32[1224]{0:T(1024)}, f32[1224]{0:T(1024)S(1)}, u32[]{:S(2)}) copy-start(f32[1224]{0:T(1024)S(1)} %broadcast_multiply_fusion) | copy-start | bytes 14692
  256.3 132.2 %copy-start.21 = (f32[1224]{0:T(1024)}, f32[1224]{0:T(1024)S(1)}, u32[]{:S(2)}) copy-start(f32[1224]{0:T(1024)S(1)} %fusion.38) | copy-start | bytes 14692
  256.3 345.0 %reduce-scatter.19.cloned.1.call-start = ((), (), s32[]{:S(2)}) async-start(), calls=%async_computation.15 | async-start | bytes 1474560 | tf_op jit(solution)/shard_map/reduce_scatter | solution.py:254
  266.9 89.3 %copy-start.4 = (bf16[1224,768]{1,0:T(8,128)(2,1)S(1)}, bf16[1224,768]{1,0:T(8,128)(2,1)}, u32[]{:S(2)}) copy-start(bf16[1224,768]{1,0:T(8,128)(2,1)} %param.22) | copy-start | bytes 5640196
  266.9 89.3 %copy-start.17 = (f32[1224]{0:T(1024)S(1)}, f32[1224]{0:T(1024)}, u32[]{:S(2)}) copy-start(f32[1224]{0:T(1024)} %fusion.36) | copy-start | bytes 14692
  398.9 204.4 %all-gather.18.cloned.1.call-start = ((), (), s32[]{:S(2)}) async-start(), calls=%async_computation.13 | async-start | bytes 4423680 | tf_op jit(solution)/shard_map/all_gather | solution.py:199
  399.7 239.5 %reduce-scatter.17.cloned.1.call-start = ((), (), s32[]{:S(2)}) async-start(), calls=%async_computation.14 | async-start | bytes 4423680 | tf_op jit(solution)/shard_map/reduce_scatter | solution.py:251
  411.3 152.6 %copy-start.1 = (bf16[1224,768]{1,0:T(8,128)(2,1)S(1)}, bf16[1224,768]{1,0:T(8,128)(2,1)}, u32[]{:S(2)}) copy-start(bf16[1224,768]{1,0:T(8,128)(2,1)} %param.20) | copy-start | bytes 5640196
  411.3 152.6 %copy-start.6 = (f32[1224]{0:T(1024)S(1)}, f32[1224]{0:T(1024)}, u32[]{:S(2)}) copy-start(f32[1224]{0:T(1024)} %copy-done.5) | copy-start | bytes 14692
  411.3 152.7 %copy-start.12 = (f32[1224]{0:T(1024)S(1)}, f32[1224]{0:T(1024)}, u32[]{:S(2)}) copy-start(f32[1224]{0:T(1024)} %copy-done.11) | copy-start | bytes 14692
  411.3 152.7 %copy-start.16 = (f32[768]{0:T(1024)S(1)}, f32[768]{0:T(1024)}, u32[]{:S(2)}) copy-start(f32[768]{0:T(1024)} %copy-done.15) | copy-start | bytes 9220
  411.3 152.7 %copy-start.27 = (f32[768]{0:T(1024)S(1)}, f32[768]{0:T(1024)}, u32[]{:S(2)}) copy-start(f32[768]{0:T(1024)} %copy-done.26) | copy-start | bytes 9220
  574.2 152.9 %reduce-scatter.21.cloned.1.call-start = ((), (), s32[]{:S(2)}) async-start(), calls=%async_computation.16 | async-start | bytes 5898240 | tf_op jit(solution)/shard_map/reduce_scatter | solution.py:257
  586.4 229.9 %reduce-scatter.23.cloned.1.call-start = ((), (), s32[]{:S(2)}) async-start(), calls=%async_computation.17 | async-start | bytes 5898240 | tf_op jit(solution)/shard_map/reduce_scatter | solution.py:260
  598.4 255.4 %reduce-scatter.27.cloned.1.call-start = ((), (), s32[]{:S(2)}) async-start(), calls=%async_computation.19 | async-start | bytes 442368
  603.3 290.4 %reduce-scatter.25.cloned.1.call-start = ((), (), s32[]{:S(2)}) async-start(), calls=%async_computation.18 | async-start | bytes 1327104
  641.5 294.3 %reduce-scatter.29.cloned.1.call-start = ((), (), s32[]{:S(2)}) async-start(), calls=%async_computation.20 | async-start | bytes 1769472
  645.4 84.3 %copy-start.20 = (f32[1224]{0:T(1024)S(1)}, f32[1224]{0:T(1024)}, u32[]{:S(2)}) copy-start(f32[1224]{0:T(1024)} %copy-done.19) | copy-start | bytes 14692
  729.6 246.4 %reduce-scatter.31.cloned.1.call-start = ((), (), s32[]{:S(2)}) async-start(), calls=%async_computation.21 | async-start | bytes 1327104
  (43 other events, 638.8 us)
Sparse Core Ops, SparseCore 0:
  10.0 27.7 all-gather.9
  39.9 50.4 all-gather.7
  92.3 31.7 all-gather.13
  180.2 86.6 all-gather.11
  268.3 87.8 all-gather.15
  399.0 27.5 reduce-scatter.18
  428.2 68.7 all-gather.17
  574.3 64.8 reduce-scatter.16
  641.5 85.5 reduce-scatter.20
  729.2 87.0 reduce-scatter.22
  819.4 34.3 reduce-scatter.26
  856.9 36.7 reduce-scatter.24
  897.3 38.4 reduce-scatter.28
  939.2 36.7 reduce-scatter.30
